TPU v7x, 256 devices: a whole 4x4x8 slice. The times are simulated.
256 devices in a mesh: dom: 16 (over y, z_hi, core), orb: 16 (over z_lo, x).
Axes of the slice: x: 4, y: 4, z: 8 (z_hi: 2, z_lo: 4; z = z_hi * 4 + z_lo), core: 2. Of those that a mesh axis runs over, the one named last changes fastest.
Arguments:
- psi: float32 [49152, 2048], P('dom', 'orb'), may hold values from -6 to 6
- rot: float32 [2048, 2048], P(None, 'orb'), may hold values from -0.125 to 0.125
- occ: float32 [2048], P('orb'), may hold values from 0.1 to 2
- v_loc: float32 [49152], P('dom'), may hold values from -1 to 1
Outputs:
- rotated: float32 [49152, 2048], P('dom', 'orb')
- density: float32 [49152], P('dom')
- hpsi: float32 [49152, 2048], P('dom', 'orb')
- band: float32 [2048], P('orb')
All inputs are finite; a program needn't handle non-finite values.
Results may differ from a plain program's by a relative error of at most 0.000075.
Values sent between devices are 32-bit elements; how exact they have to be, the bound alone decides.
A program may use at most 128 MiB of HBM per device.

v0:
```python
import jax
import jax.numpy as jnp
from jax import lax
from jax.sharding import PartitionSpec as P

M = 2048
PLANES_DEV = 3
NY = 8
NZ = 128


def with_halo(cells, sides, width):
    for axis, dim in sides:
        count = lax.axis_size(axis)
        head = lax.slice_in_dim(cells, 0, width, axis=dim)
        tail = lax.slice_in_dim(cells, cells.shape[dim] - width, cells.shape[dim], axis=dim)
        cells = jnp.concatenate(
            [
                lax.ppermute(tail, axis, [(i, (i + 1) % count) for i in range(count)]),
                cells,
                lax.ppermute(head, axis, [((i + 1) % count, i) for i in range(count)]),
            ],
            axis=dim,
        )
    return cells


def shards(psi, rot, occ, v_loc):
    points = psi.shape[0]
    local_m = psi.shape[1]
    rotated = jnp.dot(
        lax.all_gather(psi, "orb", axis=1, tiled=True),
        rot,
        precision=lax.Precision.HIGHEST,
        preferred_element_type=jnp.float32,
    )
    factor = (3.0 / jnp.pi) ** (1.0 / 3.0)
    part_density = jnp.sum(occ[None, :] * rotated * rotated, axis=1) / M
    density = lax.psum(part_density, "orb")
    potential = v_loc - factor * jnp.cbrt(density)
    field = rotated.reshape(PLANES_DEV, NY, NZ, local_m)
    padded = with_halo(field, (("dom", 0),), 1)
    beside = padded[2:] + padded[:-2]
    beside = beside + jnp.roll(field, 1, 1) + jnp.roll(field, -1, 1)
    beside = beside + jnp.roll(field, 1, 2) + jnp.roll(field, -1, 2)
    lap = (beside - 6.0 * field).reshape(points, local_m)
    hpsi = -0.5 * lap + potential[:, None] * rotated
    total_points = points * lax.axis_size("dom")
    band = lax.psum(jnp.sum(rotated * hpsi, axis=0) / total_points, "dom")
    return (rotated, density, hpsi, band)


def solution(mesh):
    placed = (P("dom", "orb"), P(None, "orb"), P("orb"), P("dom"))
    return jax.shard_map(
        shards,
        mesh=mesh,
        in_specs=placed,
        out_specs=(P("dom", "orb"), P("dom"), P("dom", "orb"), P("orb")),
        check_vma=False,
    )
```

profile of v0, /device:TPU:1, one launch (start us, length us, event | category | flops | bytes accessed | tf_op | source)
XLA Modules:
  0.0 467.3 jit_solution(15447638817102200703)
XLA Ops:
  7.2 0.0 copy-start
  7.2 0.0 copy-start.5
  7.2 0.0 all-gather.2.cloned.1.call-start
  7.2 0.7 all-gather.2.cloned.1.call-update
  7.9 273.7 %all-gather.2.cloned.1.call-done = f32[3072,2048]{1,0:T(8,128)} async-done(((f32[3072,128]{1,0:T(8,128)}), f32[3072,2048]{1,0:T(8,128)}) %all-gather.2.cloned.1.call-update) | async-done | bytes 25165840 | tf_op jit(solution)/shard_map/all_gather | solution.py:32
  281.6 0.0 copy-done
  281.6 0.0 copy-done.5
  281.6 23.2 %fusion = (f32[3072]{0:T(1024)S(1)}, f32[3072,128]{1,0:T(8,128)S(1)}) fusion(f32[128]{0:T(128)S(1)} %copy-done.5, f32[3072,2048]{1,0:T(8,128)} %all-gather.2.cloned.1.call-done, f32[2048,128]{1,0:T(8,128)S(1)} %copy-done), kind=kOutput, calls=%fused_computation.1 | convolution fusion | flops 9664852992 | bytes 27800064 | tf_op jit(solution)/shard_map/dot_general | solution.py:31
  304.9 0.0 copy-start.1
  304.9 0.7 fusion.9
  305.6 0.9 fusion.12
  306.5 1.9 fusion.10
  308.4 0.6 broadcast_multiply_fusion
  309.0 63.9 %psum.14 = f32[3072]{0:T(1024)} all-reduce(f32[3072]{0:T(1024)} %broadcast_multiply_fusion), channel_id=1, replica_groups=mesh['dom'=16,'orb'=16] {'orb'}, use_global_device_ids=true, to_apply=%region_1.0 | all-reduce | flops 3072 | bytes 24576 | tf_op jit(solution)/shard_map/psum | solution.py:39
  372.9 26.3 %collective-permute-start.1 = (f32[1,8,128,128]{3,2,1,0:T(8,128)}, f32[1,8,128,128]{3,2,1,0:T(8,128)S(1)}, u32[]{:S(2)}, u32[]{:S(2)}) collective-permute-start(f32[1,8,128,128]{3,2,1,0:T(8,128)} %bitcast.14), channel_id=1, source_target_pairs={{0,16},{16,32},{32,48},{48,64},{64,80},{80,96},{96,112},{112,128},... | collective-permute-start | bytes 1572872 | tf_op jit(solution)/shard_map/ppermute | solution.py:19
  399.1 0.0 collective-permute-start
  399.1 0.7 multiply_subtract_fusion
  399.9 0.0 copy-start.2
  399.9 0.0 copy-start.3
  399.9 0.0 copy-start.4
  399.9 0.3 fusion.8
  400.2 6.7 %collective-permute-done.1 = f32[1,8,128,128]{3,2,1,0:T(8,128)S(1)} collective-permute-done((f32[1,8,128,128]{3,2,1,0:T(8,128)}, f32[1,8,128,128]{3,2,1,0:T(8,128)S(1)}, u32[]{:S(2)}, u32[]{:S(2)}) %collective-permute-start.1) | collective-permute-done | bytes 524320 | tf_op jit(solution)/shard_map/ppermute | solution.py:19
  406.9 8.9 %collective-permute-done = f32[1,8,128,128]{3,2,1,0:T(8,128)S(1)} collective-permute-done((f32[1,8,128,128]{3,2,1,0:T(8,128)S(1)}, f32[1,8,128,128]{3,2,1,0:T(8,128)S(1)}, u32[]{:S(2)}, u32[]{:S(2)}) %collective-permute-start) | collective-permute-done | bytes 524320 | tf_op jit(solution)/shard_map/ppermute | solution.py:21
  415.8 0.0 copy-done.2
  415.8 0.0 copy-done.3
  415.8 0.0 copy-done.4
  415.8 1.1 fusion.7
  416.8 0.0 copy-done.1
  416.8 1.6 multiply_reduce_fusion
  418.5 41.9 %psum.15 = f32[128]{0:T(128)} all-reduce(f32[128]{0:T(128)S(1)} %broadcast_multiply_fusion.1), channel_id=1, replica_groups=mesh['dom'=16,'orb'=16] {'dom'}, use_global_device_ids=true, to_apply=%region_3.4 | all-reduce | flops 128 | bytes 1024 | tf_op jit(solution)/shard_map/psum | solution.py:49
  (2 shorter events, 0.0 us)
Async XLA Ops:
  7.2 274.5 %copy-start = (f32[2048,128]{1,0:T(8,128)S(1)}, f32[2048,128]{1,0:T(8,128)}, u32[]{:S(2)}) copy-start(f32[2048,128]{1,0:T(8,128)} %param.5) | copy-start | bytes 3145732
  7.2 274.4 %copy-start.5 = (f32[128]{0:T(128)S(1)}, f32[128]{0:T(128)}, u32[]{:S(2)}) copy-start(f32[128]{0:T(128)} %param.6) | copy-start | bytes 1540
  7.2 274.4 %all-gather.2.cloned.1.call-start = ((), (), s32[]{:S(2)}) async-start(), calls=%async_computation | async-start | bytes 26738688 | tf_op jit(solution)/shard_map/all_gather | solution.py:32
  304.9 112.0 %copy-start.1 = (f32[3072,128]{1,0:T(8,128)}, f32[3072,128]{1,0:T(8,128)S(1)}, u32[]{:S(2)}) copy-start(f32[3072,128]{1,0:T(8,128)S(1)} %get-tuple-element.17) | copy-start | bytes 4718596
  372.9 34.0 %collective-permute-start.1 = (f32[1,8,128,128]{3,2,1,0:T(8,128)}, f32[1,8,128,128]{3,2,1,0:T(8,128)S(1)}, u32[]{:S(2)}, u32[]{:S(2)}) collective-permute-start(f32[1,8,128,128]{3,2,1,0:T(8,128)} %bitcast.14), channel_id=1, source_target_pairs={{0,16},{16,32},{32,48},{48,64},{64,80},{80,96},{96,112},{112,128},... | collective-permute-start | bytes 1572872 | tf_op jit(solution)/shard_map/ppermute | solution.py:19
  399.1 16.6 %collective-permute-start = (f32[1,8,128,128]{3,2,1,0:T(8,128)S(1)}, f32[1,8,128,128]{3,2,1,0:T(8,128)S(1)}, u32[]{:S(2)}, u32[]{:S(2)}) collective-permute-start(f32[1,8,128,128]{3,2,1,0:T(8,128)S(1)} %bitcast.13), channel_id=1, source_target_pairs={{16,0},{32,16},{48,32},{64,48},{80,64},{96,80},{112,96},{128,112},... | collective-permute-start | bytes 1572872 | tf_op jit(solution)/shard_map/ppermute | solution.py:21
  399.9 15.9 %copy-start.2 = (f32[3,7,128,128]{3,2,1,0:T(8,128)S(1)}, f32[3,7,128,128]{3,2,1,0:T(8,128)}, u32[]{:S(2)}) copy-start(f32[3,7,128,128]{3,2,1,0:T(8,128)} %get-tuple-element.10) | copy-start | bytes 4128772
  399.9 15.9 %copy-start.3 = (f32[3,7,128,128]{3,2,1,0:T(8,128)S(1)}, f32[3,7,128,128]{3,2,1,0:T(8,128)}, u32[]{:S(2)}) copy-start(f32[3,7,128,128]{3,2,1,0:T(8,128)} %get-tuple-element.11) | copy-start | bytes 4128772
  399.9 15.9 %copy-start.4 = (f32[3,8,1,128]{3,2,1,0:T(1,128)S(1)}, f32[3,8,1,128]{3,2,1,0:T(1,128)}, u32[]{:S(2)}) copy-start(f32[3,8,1,128]{3,2,1,0:T(1,128)} %get-tuple-element.9) | copy-start | bytes 36868
Sparse Core Ops, SparseCore 0:
  9.7 271.8 all-gather.1
where the time goes:
time: 474 us; the launch traced here: 467 us
  waiting for transfers between devices  290 us (61%)
  blocking collectives  106 us (22%)
  starting transfers between devices  26.3 us (6%)
  matrix products  23.2 us (5%)
  between operations  14.1 us (3%)
    all_gather x1, waiting for transfers between devices, shards(): lax.all_gather(psi, 'orb', axis=1, tiled=True)  274 us
    psum x1, blocking collectives, shards(): density = lax.psum(part_density, 'orb')  63.9 us
    psum x1, blocking collectives, shards(): band = lax.psum(jnp.sum(rotated * hpsi, axis=0) / total_points, 'dom')  41.9 us
    ppermute x1, starting transfers between devices, with_halo(): lax.ppermute(tail, axis, [(i, (i + 1) % count) for i in range(count)])  26.3 us
    dot_general x1, matrix products, shards(): jnp.dot(lax.all_gather(psi, 'orb', axis=1, tiled=True), rot, precision=la...  23.2 us
  transfers between devices with their start and end apart: 3, of which 3 were waited for; matrix products, arithmetic and copies ran while one was open for 0% of the time, Pallas kernels for 0%

commit v1 on v0

v1 whole, which is shorter than its diff:
```python
import functools

import jax
import jax.numpy as jnp
from jax import lax
from jax.experimental import pallas as pl
from jax.experimental.pallas import tpu as pltpu
from jax.sharding import PartitionSpec as P

M = 2048
PTS = 3072
NORB = 128
NLINE = 24
LINE = 128
NPTS = 49152
AHEAD = 3
LAG_C = 2
LAG_D = 4
LAG_E = 6
MESH = pl.DeviceIdType.MESH
HIGHEST = lax.Precision.HIGHEST


def line_of(k):
    q = k // 8
    return (2 * q - 3 * (q // 2)) * 8 + k % 8


def split(v):
    hi = v.astype(jnp.bfloat16)
    return hi, (v - hi.astype(jnp.float32)).astype(jnp.bfloat16)


def cbrt(d):
    safe = jnp.maximum(d, 1e-37)
    y = jnp.exp(jnp.log(safe) * (1.0 / 3.0))
    y = y - (y - safe / (y * y)) * (1.0 / 3.0)
    return jnp.where(d < 1e-37, 0.0, y)


def kernel(psi, rot, occ, vloc, rotated, dens, hpsi, band,
           abuf, rotv, rbuf, bhi, blo, part, rsb, halo, dpart, dx, dsum, dz, bpart, b1, bsum, b2,
           in_sem, a_recv, a_send, rs_recv, rs_send, h_recv, h_send, r1_sem, r2_send, r2_recv,
           d_send, d_recv, b_send, b_recv):
    dom = lax.axis_index("dom")
    orb = lax.axis_index("orb")
    y, zh, c = dom // 4, (dom // 2) % 2, dom % 2
    z, x = orb // 4, orb % 4
    z1, z0 = z // 2, z % 2
    xp, xm, xo = (x + 1) % 4, (x + 3) % 4, (x + 2) % 4
    at_xp, at_xm = (dom, z * 4 + xp), (dom, z * 4 + xm)
    at_z0 = (dom, (z1 * 2 + 1 - z0) * 4 + x)
    at_z1 = (dom, ((1 - z1) * 2 + z0) * 4 + x)
    at_prev, at_next = ((dom + 15) % 16, orb), ((dom + 1) % 16, orb)
    e = y * 2 + c

    def at_yc(f):
        return ((f // 2) * 4 + zh * 2 + f % 2, orb)

    x_peers = [(dom, z * 4 + (x + j) % 4) for j in (1, 2, 3)]
    z_peers = [(dom, ((z + j) % 4) * 4 + x) for j in (1, 2, 3)]
    yc_peers = [at_yc((e + j) % 8) for j in range(1, 8)]
    s = zh * 2 + c
    zc_peers = [(y * 4 + (s + j) % 4, orb) for j in (1, 2, 3)]
    y_peers = [(((y + j) % 4) * 4 + s, orb) for j in (1, 2, 3)]

    own, pb = z0 * 4 + x, (1 - z0) * 4 + x
    load_psi = pltpu.make_async_copy(psi, abuf.at[own], in_sem.at[0])
    load_psi.start()
    load_rot = pltpu.make_async_copy(rot, rotv, in_sem.at[1])
    load_rot.start()

    barrier = pltpu.get_barrier_semaphore()
    everyone = x_peers + z_peers + yc_peers + zc_peers + [at_prev, at_next]
    for peer in everyone:
        pl.semaphore_signal(barrier, inc=1, device_id=peer, device_id_type=MESH)
    pl.semaphore_wait(barrier, len(everyone))
    load_psi.wait()
    load_rot.wait()

    def remote(src, dst, send, recv, peer):
        return pltpu.make_async_remote_copy(
            src_ref=src, dst_ref=dst, send_sem=send, recv_sem=recv, device_id=peer, device_id_type=MESH)

    def rows_of(k):
        return pl.ds(pl.multiple_of(line_of(k) * LINE, LINE), LINE)

    def block(b, k, way, peer):
        ref = abuf.at[b, rows_of(k)]
        return remote(ref, ref, a_send.at[way], a_recv.at[b, k], peer)

    def got(b, k):
        block(b, k, 0, at_xp).wait_recv()

    def send_own(k):
        block(own, k, 0, at_z0).start()
        block(own, k, 1, at_xp).start()
        block(own, k, 2, at_xm).start()

    send_r1 = remote(
        rotv.at[pl.ds(pl.multiple_of((1 - z1) * 1024 + e * 128, 128), 128)], rbuf.at[e],
        r1_sem.at[0], r1_sem.at[1], at_z1)
    send_r1.start()
    for k in range(AHEAD):
        send_own(k)

    def share(j):
        return remote(rbuf.at[e], rbuf.at[e], r2_send.at[j], r2_recv.at[e], yc_peers[j])

    def rs_copy(k):
        rows = rows_of(k)
        return remote(part.at[rows], rsb.at[rows], rs_send.at[0], rs_recv.at[k], at_z1)

    def step(i, _):
        @pl.when(i + AHEAD < NLINE)
        def _():
            send_own(i + AHEAD)

        @pl.when(i < NLINE)
        def _():
            got(pb, i)
            block(pb, i, 3, at_xp).start()
            block(pb, i, 4, at_xm).start()
            got(z0 * 4 + xm, i)
            block(z0 * 4 + xm, i, 5, at_xp).start()

        @pl.when(i == 0)
        def _():
            send_r1.wait_recv()
            for j in range(7):
                share(j).start()

        @pl.when((i >= LAG_C) & (i < NLINE + LAG_C))
        def _():
            k = i - LAG_C
            got((1 - z0) * 4 + xp, k)
            block((1 - z0) * 4 + xp, k, 6, at_xm).start()

        @pl.when(i == LAG_D)
        def _():
            for j in range(1, 8):
                f = (e + j) % 8
                remote(rbuf.at[f], rbuf.at[f], r2_send.at[0], r2_recv.at[f], at_z1).wait_recv()
            hi, lo = split(rotv[pl.ds(pl.multiple_of(z1 * 1024, 1024), 1024), :])
            bhi[:, :NORB] = hi
            blo[:, :NORB] = lo
            hi, lo = split(rbuf[...].reshape(1024, NORB))
            bhi[:, NORB:] = hi
            blo[:, NORB:] = lo

        @pl.when((i >= LAG_D) & (i < NLINE + LAG_D))
        def _():
            k = i - LAG_D
            got((1 - z0) * 4 + xm, k)
            got(z0 * 4 + xp, k)
            got(z0 * 4 + xo, k)
            got((1 - z0) * 4 + xo, k)
            rows = rows_of(k)
            a = jnp.concatenate([abuf[b, rows, :] for b in range(8)], axis=1)
            hi, lo = split(a)
            total = jnp.dot(hi, blo[...], preferred_element_type=jnp.float32)
            total += jnp.dot(lo, bhi[...], preferred_element_type=jnp.float32)
            total += jnp.dot(hi, bhi[...], preferred_element_type=jnp.float32)
            rotated[rows, :] = total[:, :NORB]
            part[rows, :] = total[:, NORB:]

        @pl.when((i >= LAG_E + 1) & (i < 16 + LAG_E + 1))
        def _():
            k = i - LAG_E - 1
            rows = rows_of(k)
            there = pl.ds(pl.multiple_of((k % 8) * LINE, LINE), LINE)

            @pl.when(k < 8)
            def _():
                remote(rotated.at[rows], halo.at[1, there], h_send.at[0], h_recv.at[1], at_prev).start()

            @pl.when(k >= 8)
            def _():
                remote(rotated.at[rows], halo.at[0, there], h_send.at[1], h_recv.at[0], at_next).start()

        @pl.when((i >= LAG_E) & (i < NLINE + LAG_E))
        def _():
            k = i - LAG_E
            rs_copy(k).wait_recv()
            rows = rows_of(k)
            r = rotated[rows, :] + rsb[rows, :]
            rotated[rows, :] = r
            d = lax.dot_general(jnp.broadcast_to(occ[...], (8, NORB)), r * r, (((1,), (1,)), ((), ())),
                                precision=HIGHEST, preferred_element_type=jnp.float32)
            dpart[pl.ds(line_of(k), 1), :] = d[0:1]

        @pl.when((i >= LAG_D) & (i < NLINE + LAG_D))
        def _():
            rs_copy(i - LAG_D).start()

        return 0

    lax.fori_loop(0, NLINE + LAG_E, step, 0)

    for way, peer in enumerate([at_z0, at_xp, at_xm, at_xp, at_xm, at_xp, at_xm]):
        remote(abuf.at[own], abuf.at[own], a_send.at[way], a_recv.at[0, 0], peer).wait_send()

    def exchange(src, dst, send, recv, base, peers):
        return [remote(src, dst.at[2 - j], send.at[base + j], recv.at[base + 2 - j], peer)
                for j, peer in enumerate(peers)]

    stage = exchange(dpart, dx, d_send, d_recv, 0, x_peers)
    for copy in stage:
        copy.start()

    remote(halo.at[0], halo.at[0], h_send.at[0], h_recv.at[0], at_next).wait_recv()
    remote(halo.at[1], halo.at[1], h_send.at[0], h_recv.at[1], at_next).wait_recv()

    def beside_line(p, line):
        rows = pl.ds(line * LINE, LINE)
        r = rotated[pl.ds((p * 8 + line) * LINE, LINE), :]
        below = rotated[pl.ds(((p - 1) * 8 + line) * LINE, LINE), :] if p > 0 else halo[0, rows, :]
        above = rotated[pl.ds(((p + 1) * 8 + line) * LINE, LINE), :] if p < 2 else halo[1, rows, :]
        total = below + above
        total += rotated[pl.ds((p * 8 + (line + 1) % 8) * LINE, LINE), :]
        total += rotated[pl.ds((p * 8 + (line + 7) % 8) * LINE, LINE), :]
        total += pltpu.roll(r, 1, 0) + pltpu.roll(r, LINE - 1, 0)
        return r, 3.0 * r - 0.5 * total

    acc = jnp.zeros((8, NORB), jnp.float32)
    for p in range(3):
        for line in range(8):
            r, h = beside_line(p, line)
            hpsi[pl.ds((p * 8 + line) * LINE, LINE), :] = h
            acc += jnp.sum((r * h).reshape(LINE // 8, 8, NORB), axis=0)

    for copy in stage:
        copy.wait_recv()
    dsum[...] = dpart[...] + dx[0] + dx[1] + dx[2]
    for copy in stage:
        copy.wait_send()
    stage = exchange(dsum, dz, d_send, d_recv, 3, z_peers)
    for copy in stage:
        copy.start()
    for copy in stage:
        copy.wait_recv()
    density = (dsum[...] + dz[0] + dz[1] + dz[2]) * (1.0 / M)
    for copy in stage:
        copy.wait_send()
    dens[...] = density
    pot = vloc[...] - (3.0 / jnp.pi) ** (1.0 / 3.0) * cbrt(density)

    extra = jnp.zeros((8, NORB), jnp.float32)
    for n in range(NLINE):
        r = rotated[pl.ds(n * LINE, LINE), :]
        extra += jnp.dot(jnp.broadcast_to(pot[n:n + 1], (8, LINE)), r * r,
                         precision=HIGHEST, preferred_element_type=jnp.float32)
    mine = jnp.sum(acc, axis=0, keepdims=True) + extra[0:1]
    bpart[...] = jnp.broadcast_to(mine, (8, NORB))
    stage = exchange(bpart, b1, b_send, b_recv, 0, zc_peers)
    for copy in stage:
        copy.start()

    for n in range(NLINE):
        rows = pl.ds(n * LINE, LINE)
        column = jnp.broadcast_to(pot[n:n + 1], (LINE, LINE)).T
        hpsi[rows, :] = hpsi[rows, :] + column * rotated[rows, :]

    for copy in stage:
        copy.wait_recv()
    bsum[...] = bpart[...] + b1[0] + b1[1] + b1[2]
    for copy in stage:
        copy.wait_send()
    stage = exchange(bsum, b2, b_send, b_recv, 3, y_peers)
    for copy in stage:
        copy.start()
    for copy in stage:
        copy.wait_recv()
    band[...] = ((bsum[...] + b2[0] + b2[1] + b2[2]) * (1.0 / NPTS))[0:1]
    for copy in stage:
        copy.wait_send()

    send_r1.wait_send()
    for j in range(7):
        share(j).wait_send()
    whole = pl.ds(0, PTS)
    remote(part.at[whole], rsb.at[whole], rs_send.at[0], rs_recv.at[0], at_z1).wait_send()
    for side in range(2):
        remote(halo.at[0], halo.at[0], h_send.at[side], h_recv.at[0], at_next).wait_send()


def shards(psi, rot, occ, v_loc):
    f32 = jnp.float32
    vmem, hbm = pl.BlockSpec(memory_space=pltpu.VMEM), pl.BlockSpec(memory_space=pl.ANY)
    dma = pltpu.SemaphoreType.DMA
    rotated, density, hpsi, band = pl.pallas_call(
        kernel,
        out_shape=(
            jax.ShapeDtypeStruct((PTS, NORB), f32),
            jax.ShapeDtypeStruct((NLINE, LINE), f32),
            jax.ShapeDtypeStruct((PTS, NORB), f32),
            jax.ShapeDtypeStruct((1, NORB), f32),
        ),
        in_specs=[hbm, hbm, vmem, vmem],
        out_specs=(vmem, vmem, vmem, vmem),
        scratch_shapes=[
            pltpu.VMEM((8, PTS, NORB), f32),
            pltpu.VMEM((M, NORB), f32),
            pltpu.VMEM((8, 128, NORB), f32),
            pltpu.VMEM((1024, 2 * NORB), jnp.bfloat16),
            pltpu.VMEM((1024, 2 * NORB), jnp.bfloat16),
            pltpu.VMEM((PTS, NORB), f32),
            pltpu.VMEM((PTS, NORB), f32),
            pltpu.VMEM((2, 1024, NORB), f32),
            pltpu.VMEM((NLINE, LINE), f32),
            pltpu.VMEM((3, NLINE, LINE), f32),
            pltpu.VMEM((NLINE, LINE), f32),
            pltpu.VMEM((3, NLINE, LINE), f32),
            pltpu.VMEM((8, NORB), f32),
            pltpu.VMEM((3, 8, NORB), f32),
            pltpu.VMEM((8, NORB), f32),
            pltpu.VMEM((3, 8, NORB), f32),
            dma((2,)),
            dma((8, NLINE)),
            dma((7,)),
            dma((NLINE,)),
            dma((1,)),
            dma((2,)),
            dma((2,)),
            dma((2,)),
            dma((7,)),
            dma((8,)),
            dma((6,)),
            dma((6,)),
            dma((6,)),
            dma((6,)),
        ],
        compiler_params=pltpu.CompilerParams(
            collective_id=0, has_side_effects=True, vmem_limit_bytes=56 * 1024 * 1024),
        name="rotate",
    )(psi, rot, occ.reshape(1, NORB), v_loc.reshape(NLINE, LINE))
    return rotated, density.reshape(PTS), hpsi, band.reshape(NORB)


def solution(mesh):
    placed = (P("dom", "orb"), P(None, "orb"), P("orb"), P("dom"))
    return jax.shard_map(
        shards,
        mesh=mesh,
        in_specs=placed,
        out_specs=(P("dom", "orb"), P("dom"), P("dom", "orb"), P("orb")),
        check_vma=False,
    )
```

time: 474 us -> 151 us (0.32); the launches traced: 467 us -> 150 us
  waiting for transfers between devices: 290 us -> 0 us
  Pallas kernels: 0 us -> 145 us
  blocking collectives: 106 us -> 0 us
  starting transfers between devices: 26.3 us -> 0 us
  matrix products: 23.2 us -> 0 us
  between operations: 14.1 us -> 0.66 us
    all_gather x1 -> x0, waiting for transfers between devices: 274 us -> none  [shards(): lax.all_gather(psi, 'orb', axis=1, tiled=True)]
    pallas_call x0 -> x1, Pallas kernels: none -> 145 us  [shards(): pl.pallas_call(kernel, out_shape=(jax.ShapeDtypeStruct((PTS, NORB), f32),...]
    psum x2 -> x0, blocking collectives: 106 us -> none  [the longest x1 63.9 us: shards(): density = lax.psum(part_density, 'orb')]
    ppermute x2 -> x0, starting transfers between devices: 26.3 us -> none  [the longest x1 26.3 us: with_halo(): lax.ppermute(tail, axis, [(i, (i + 1) % count) for i in range(count)])]
    dot_general x1 -> x0, matrix products: 23.2 us -> none  [shards(): jnp.dot(lax.all_gather(psi, 'orb', axis=1, tiled=True), rot, precision=la...]
    ppermute x2 -> x0, waiting for transfers between devices: 15.5 us -> none  [the longest x1 8.86 us: with_halo(): lax.ppermute(head, axis, [((i + 1) % count, i) for i in range(count)])]
    unnamed x12 -> x10, local copies, waits for them, and re-layouts: 0.04 us -> 5.04 us
  transfers between devices with their start and end apart: 3 -> 0, of which waited for: 3 -> 0; matrix products, arithmetic and copies ran while one was open for 0% -> 0% of each run, Pallas kernels for 0% -> 0%
where the time goes in v1:
time: 151 us; the launch traced here: 150 us
  Pallas kernels  145 us (96%)
  local copies, waits for them, and re-layouts  5.04 us (3%)
    pallas_call x1, Pallas kernels, shards(): pl.pallas_call(kernel, out_shape=(jax.ShapeDtypeStruct((PTS, NORB), f32),...  145 us
    unnamed x10, local copies, waits for them, and re-layouts  5.04 us

profile of v1, /device:TPU:1, one launch (start us, length us, event | category | flops | bytes accessed | tf_op | source)
XLA Modules:
  0.0 150.5 jit_solution(4469155477045205562)
XLA Ops:
  0.6 144.8 %rotate.1 = (f32[3072,128]{1,0:T(8,128)}, f32[24,128]{1,0:T(8,128)}, f32[3072,128]{1,0:T(8,128)}, f32[1,128]{1,0:T(1,128)}) custom-call(f32[3072,128]{1,0:T(8,128)} %psi.1, f32[2048,128]{1,0:T(8,128)} %rot.1, f32[1,128]{1,0:T(1,128)} %bitcast.6, f32[24,128]{1,0:T(8,128)} %bitcast.4), custom_call_target="tpu_custom_call" | custom-call | tf_op jit(solution)/shard_map/rotate/pallas_call | solution.py:291
  145.4 0.0 copy-start.1
  145.4 0.0 copy-start
  145.4 2.8 %copy.12 = f32[3072,128]{1,0:T(8,128)} copy(f32[3072,128]{1,0:T(8,128)} %get-tuple-element.16) | data formatting | bytes 3145728
  148.2 0.0 copy-done.1
  148.2 0.6 copy.13
  148.8 0.0 copy-done
  148.8 0.0 copy-start.2
  148.8 1.1 copy.14
  150.0 0.0 copy-done.2
  150.0 0.5 copy.15
Async XLA Ops:
  145.4 2.8 %copy-start.1 = (f32[24,128]{1,0:T(8,128)S(1)}, f32[24,128]{1,0:T(8,128)}, u32[]{:S(2)}) copy-start(f32[24,128]{1,0:T(8,128)} %get-tuple-element.9) | copy-start | bytes 36868
  145.4 3.4 %copy-start = (f32[3072,128]{1,0:T(8,128)S(1)}, f32[3072,128]{1,0:T(8,128)}, u32[]{:S(2)}) copy-start(f32[3072,128]{1,0:T(8,128)} %get-tuple-element.18) | copy-start | bytes 4718596
  148.8 1.1 copy-start.2

commit v2 on v1

--- a/solution.py
+++ b/solution.py
@@ -14,9 +14,9 @@
 LINE = 128
 NPTS = 49152
 AHEAD = 3
-LAG_C = 2
-LAG_D = 4
-LAG_E = 6
+LAG_C = 1
+LAG_D = 2
+LAG_E = 4
 MESH = pl.DeviceIdType.MESH
 HIGHEST = lax.Precision.HIGHEST
 
@@ -38,8 +38,8 @@
     return jnp.where(d < 1e-37, 0.0, y)
 
 
-def kernel(psi, rot, occ, vloc, rotated, dens, hpsi, band,
-           abuf, rotv, rbuf, bhi, blo, part, rsb, halo, dpart, dx, dsum, dz, bpart, b1, bsum, b2,
+def kernel(psi, rot, occ_hbm, vloc_hbm, rotated, dens, hpsi, band,
+           occ, vloc, abuf, rotv, rbuf, bhi, blo, part, rsb, halo, dpart, dxa, dxb, bpart, bx,
            in_sem, a_recv, a_send, rs_recv, rs_send, h_recv, h_send, r1_sem, r2_send, r2_recv,
            d_send, d_recv, b_send, b_recv):
     dom = lax.axis_index("dom")
@@ -57,26 +57,23 @@
     def at_yc(f):
         return ((f // 2) * 4 + zh * 2 + f % 2, orb)
 
-    x_peers = [(dom, z * 4 + (x + j) % 4) for j in (1, 2, 3)]
-    z_peers = [(dom, ((z + j) % 4) * 4 + x) for j in (1, 2, 3)]
+    orb_peers = [(dom, (orb + j) % 16) for j in range(1, 16)]
+    dom_peers = [((dom + j) % 16, orb) for j in range(1, 16)]
     yc_peers = [at_yc((e + j) % 8) for j in range(1, 8)]
-    s = zh * 2 + c
-    zc_peers = [(y * 4 + (s + j) % 4, orb) for j in (1, 2, 3)]
-    y_peers = [(((y + j) % 4) * 4 + s, orb) for j in (1, 2, 3)]
 
     own, pb = z0 * 4 + x, (1 - z0) * 4 + x
-    load_psi = pltpu.make_async_copy(psi, abuf.at[own], in_sem.at[0])
-    load_psi.start()
-    load_rot = pltpu.make_async_copy(rot, rotv, in_sem.at[1])
-    load_rot.start()
+    loads = [pltpu.make_async_copy(src, dst, in_sem.at[n]) for n, (src, dst) in enumerate(
+        [(psi, abuf.at[own]), (rot, rotv), (occ_hbm, occ), (vloc_hbm, vloc)])]
+    for load in loads:
+        load.start()
 
     barrier = pltpu.get_barrier_semaphore()
-    everyone = x_peers + z_peers + yc_peers + zc_peers + [at_prev, at_next]
+    everyone = orb_peers + dom_peers
     for peer in everyone:
         pl.semaphore_signal(barrier, inc=1, device_id=peer, device_id_type=MESH)
     pl.semaphore_wait(barrier, len(everyone))
-    load_psi.wait()
-    load_rot.wait()
+    for load in loads:
+        load.wait()
 
     def remote(src, dst, send, recv, peer):
         return pltpu.make_async_remote_copy(
@@ -110,6 +107,13 @@
     def rs_copy(k):
         rows = rows_of(k)
         return remote(part.at[rows], rsb.at[rows], rs_send.at[0], rs_recv.at[k], at_z1)
+
+    def to_all(src, dst, send, recv, peers):
+        for j, peer in enumerate(peers):
+            remote(src, dst.at[14 - j], send, recv, peer).start()
+
+    def from_all(dst, send, recv, peers):
+        return remote(dst, dst, send, recv, peers[0])
 
     def step(i, _):
         @pl.when(i + AHEAD < NLINE)
@@ -187,11 +191,15 @@
             rotated[rows, :] = r
             d = lax.dot_general(jnp.broadcast_to(occ[...], (8, NORB)), r * r, (((1,), (1,)), ((), ())),
                                 precision=HIGHEST, preferred_element_type=jnp.float32)
-            dpart[pl.ds(line_of(k), 1), :] = d[0:1]
+            dpart[pl.ds(k, 1), :] = d[0:1]
 
         @pl.when((i >= LAG_D) & (i < NLINE + LAG_D))
         def _():
             rs_copy(i - LAG_D).start()
+
+        @pl.when(i == LAG_E + 17)
+        def _():
+            to_all(dpart.at[pl.ds(0, 16)], dxa, d_send.at[0], d_recv.at[0], orb_peers)
 
         return 0
 
@@ -200,80 +208,52 @@
     for way, peer in enumerate([at_z0, at_xp, at_xm, at_xp, at_xm, at_xp, at_xm]):
         remote(abuf.at[own], abuf.at[own], a_send.at[way], a_recv.at[0, 0], peer).wait_send()
 
-    def exchange(src, dst, send, recv, base, peers):
-        return [remote(src, dst.at[2 - j], send.at[base + j], recv.at[base + 2 - j], peer)
-                for j, peer in enumerate(peers)]
-
-    stage = exchange(dpart, dx, d_send, d_recv, 0, x_peers)
-    for copy in stage:
-        copy.start()
+    to_all(dpart.at[pl.ds(16, 8)], dxb, d_send.at[1], d_recv.at[1], orb_peers)
 
     remote(halo.at[0], halo.at[0], h_send.at[0], h_recv.at[0], at_next).wait_recv()
     remote(halo.at[1], halo.at[1], h_send.at[0], h_recv.at[1], at_next).wait_recv()
 
-    def beside_line(p, line):
-        rows = pl.ds(line * LINE, LINE)
-        r = rotated[pl.ds((p * 8 + line) * LINE, LINE), :]
-        below = rotated[pl.ds(((p - 1) * 8 + line) * LINE, LINE), :] if p > 0 else halo[0, rows, :]
-        above = rotated[pl.ds(((p + 1) * 8 + line) * LINE, LINE), :] if p < 2 else halo[1, rows, :]
-        total = below + above
-        total += rotated[pl.ds((p * 8 + (line + 1) % 8) * LINE, LINE), :]
-        total += rotated[pl.ds((p * 8 + (line + 7) % 8) * LINE, LINE), :]
-        total += pltpu.roll(r, 1, 0) + pltpu.roll(r, LINE - 1, 0)
-        return r, 3.0 * r - 0.5 * total
-
-    acc = jnp.zeros((8, NORB), jnp.float32)
     for p in range(3):
         for line in range(8):
-            r, h = beside_line(p, line)
-            hpsi[pl.ds((p * 8 + line) * LINE, LINE), :] = h
-            acc += jnp.sum((r * h).reshape(LINE // 8, 8, NORB), axis=0)
-
-    for copy in stage:
-        copy.wait_recv()
-    dsum[...] = dpart[...] + dx[0] + dx[1] + dx[2]
-    for copy in stage:
-        copy.wait_send()
-    stage = exchange(dsum, dz, d_send, d_recv, 3, z_peers)
-    for copy in stage:
-        copy.start()
-    for copy in stage:
-        copy.wait_recv()
-    density = (dsum[...] + dz[0] + dz[1] + dz[2]) * (1.0 / M)
-    for copy in stage:
-        copy.wait_send()
+            rows = pl.ds(line * LINE, LINE)
+            here = pl.ds((p * 8 + line) * LINE, LINE)
+            r = rotated[here, :]
+            total = rotated[pl.ds(((p - 1) * 8 + line) * LINE, LINE), :] if p > 0 else halo[0, rows, :]
+            total += rotated[pl.ds(((p + 1) * 8 + line) * LINE, LINE), :] if p < 2 else halo[1, rows, :]
+            total += rotated[pl.ds((p * 8 + (line + 1) % 8) * LINE, LINE), :]
+            total += rotated[pl.ds((p * 8 + (line + 7) % 8) * LINE, LINE), :]
+            total += pltpu.roll(r, 1, 0) + pltpu.roll(r, LINE - 1, 0)
+            hpsi[here, :] = 3.0 * r - 0.5 * total
+
+    from_all(dxa, d_send.at[0], d_recv.at[0], orb_peers).wait_recv()
+    from_all(dxb, d_send.at[1], d_recv.at[1], orb_peers).wait_recv()
+    first, last = dpart[0:16], dpart[16:24]
+    for j in range(15):
+        first += dxa[j]
+        last += dxb[j]
+    density = jnp.concatenate([first[0:8], last, first[8:16]], axis=0) * (1.0 / M)
     dens[...] = density
     pot = vloc[...] - (3.0 / jnp.pi) ** (1.0 / 3.0) * cbrt(density)
-
-    extra = jnp.zeros((8, NORB), jnp.float32)
-    for n in range(NLINE):
-        r = rotated[pl.ds(n * LINE, LINE), :]
-        extra += jnp.dot(jnp.broadcast_to(pot[n:n + 1], (8, LINE)), r * r,
-                         precision=HIGHEST, preferred_element_type=jnp.float32)
-    mine = jnp.sum(acc, axis=0, keepdims=True) + extra[0:1]
-    bpart[...] = jnp.broadcast_to(mine, (8, NORB))
-    stage = exchange(bpart, b1, b_send, b_recv, 0, zc_peers)
-    for copy in stage:
-        copy.start()
-
+    turned = jnp.concatenate([pot, jnp.zeros((LINE - NLINE, LINE), jnp.float32)], axis=0).T
+
+    acc = jnp.zeros((8, NORB), jnp.float32)
     for n in range(NLINE):
         rows = pl.ds(n * LINE, LINE)
-        column = jnp.broadcast_to(pot[n:n + 1], (LINE, LINE)).T
-        hpsi[rows, :] = hpsi[rows, :] + column * rotated[rows, :]
-
-    for copy in stage:
-        copy.wait_recv()
-    bsum[...] = bpart[...] + b1[0] + b1[1] + b1[2]
-    for copy in stage:
-        copy.wait_send()
-    stage = exchange(bsum, b2, b_send, b_recv, 3, y_peers)
-    for copy in stage:
-        copy.start()
-    for copy in stage:
-        copy.wait_recv()
-    band[...] = ((bsum[...] + b2[0] + b2[1] + b2[2]) * (1.0 / NPTS))[0:1]
-    for copy in stage:
-        copy.wait_send()
+        r = rotated[rows, :]
+        h = hpsi[rows, :] + jnp.broadcast_to(turned[:, n:n + 1], (LINE, NORB)) * r
+        hpsi[rows, :] = h
+        acc += jnp.sum((r * h).reshape(LINE // 8, 8, NORB), axis=0)
+    bpart[...] = acc
+    from_all(dxa, d_send.at[0], d_recv.at[0], orb_peers).wait_send()
+    from_all(dxb, d_send.at[1], d_recv.at[1], orb_peers).wait_send()
+    to_all(bpart, bx, b_send.at[0], b_recv.at[0], dom_peers)
+    shared = from_all(bx, b_send.at[0], b_recv.at[0], dom_peers)
+    shared.wait_recv()
+    total = acc
+    for j in range(15):
+        total += bx[j]
+    band[...] = jnp.sum(total, axis=0, keepdims=True) * (1.0 / NPTS)
+    shared.wait_send()
 
     send_r1.wait_send()
     for j in range(7):
@@ -284,9 +264,32 @@
         remote(halo.at[0], halo.at[0], h_send.at[side], h_recv.at[0], at_next).wait_send()
 
 
+def put_kernel(*refs):
+    count = len(refs) // 2
+    sem = refs[-1]
+    copies = [pltpu.make_async_copy(refs[n], refs[count + n], sem.at[n]) for n in range(count)]
+    for copy in copies:
+        copy.start()
+    for copy in copies:
+        copy.wait()
+
+
+def put(*arrays):
+    hbm = pl.BlockSpec(memory_space=pl.ANY)
+    return pl.pallas_call(
+        put_kernel,
+        out_shape=tuple(jax.ShapeDtypeStruct(a.shape, a.dtype) for a in arrays),
+        in_specs=[hbm] * len(arrays),
+        out_specs=(hbm,) * len(arrays),
+        scratch_shapes=[pltpu.SemaphoreType.DMA((len(arrays),))],
+        compiler_params=pltpu.CompilerParams(vmem_limit_bytes=16 * 1024 * 1024),
+        name="put",
+    )(*arrays)
+
+
 def shards(psi, rot, occ, v_loc):
     f32 = jnp.float32
-    vmem, hbm = pl.BlockSpec(memory_space=pltpu.VMEM), pl.BlockSpec(memory_space=pl.ANY)
+    vmem, hbm = pl.BlockSpec(memory_space=pltpu.VMEM), pl.BlockSpec(memory_space=pltpu.HBM)
     dma = pltpu.SemaphoreType.DMA
     rotated, density, hpsi, band = pl.pallas_call(
         kernel,
@@ -296,9 +299,11 @@
             jax.ShapeDtypeStruct((PTS, NORB), f32),
             jax.ShapeDtypeStruct((1, NORB), f32),
         ),
-        in_specs=[hbm, hbm, vmem, vmem],
+        in_specs=[hbm] * 4,
         out_specs=(vmem, vmem, vmem, vmem),
         scratch_shapes=[
+            pltpu.VMEM((1, NORB), f32),
+            pltpu.VMEM((NLINE, LINE), f32),
             pltpu.VMEM((8, PTS, NORB), f32),
             pltpu.VMEM((M, NORB), f32),
             pltpu.VMEM((8, 128, NORB), f32),
@@ -308,14 +313,11 @@
             pltpu.VMEM((PTS, NORB), f32),
             pltpu.VMEM((2, 1024, NORB), f32),
             pltpu.VMEM((NLINE, LINE), f32),
-            pltpu.VMEM((3, NLINE, LINE), f32),
-            pltpu.VMEM((NLINE, LINE), f32),
-            pltpu.VMEM((3, NLINE, LINE), f32),
+            pltpu.VMEM((15, 16, LINE), f32),
+            pltpu.VMEM((15, 8, LINE), f32),
             pltpu.VMEM((8, NORB), f32),
-            pltpu.VMEM((3, 8, NORB), f32),
-            pltpu.VMEM((8, NORB), f32),
-            pltpu.VMEM((3, 8, NORB), f32),
-            dma((2,)),
+            pltpu.VMEM((15, 8, NORB), f32),
+            dma((4,)),
             dma((8, NLINE)),
             dma((7,)),
             dma((NLINE,)),
@@ -325,16 +327,17 @@
             dma((2,)),
             dma((7,)),
             dma((8,)),
-            dma((6,)),
-            dma((6,)),
-            dma((6,)),
-            dma((6,)),
+            dma((2,)),
+            dma((2,)),
+            dma((1,)),
+            dma((1,)),
         ],
         compiler_params=pltpu.CompilerParams(
-            collective_id=0, has_side_effects=True, vmem_limit_bytes=56 * 1024 * 1024),
+            collective_id=0, has_side_effects=True, vmem_limit_bytes=40 * 1024 * 1024),
         name="rotate",
-    )(psi, rot, occ.reshape(1, NORB), v_loc.reshape(NLINE, LINE))
-    return rotated, density.reshape(PTS), hpsi, band.reshape(NORB)
+    )(*[pltpu.with_memory_space_constraint(v, pltpu.HBM) for v in (
+        psi, rot, occ.reshape(1, NORB), v_loc.reshape(NLINE, LINE))])
+    return put(rotated, density.reshape(PTS), hpsi, band.reshape(NORB))
 
 
 def solution(mesh):

time: 151 us -> 142 us (0.940)
  local copies, waits for them, and re-layouts: 5.04 us -> 0 us
  Pallas kernels: 145 us -> 141 us
    pallas_call x1, Pallas kernels: 145 us -> 139 us  [shards(): pl.pallas_call(kernel, out_shape=(jax.ShapeDtypeStruct((PTS, NORB), f32),...]
    unnamed x10 -> x0, local copies, waits for them, and re-layouts: 5.04 us -> none
    pallas_call x0 -> x1, Pallas kernels: none -> 1.7 us  [put(): pl.pallas_call(put_kernel, out_shape=tuple((jax.ShapeDtypeStruct(a.shape,...]
where the time goes in v2:
time: 142 us
  Pallas kernels  141 us (99%)
    pallas_call x1, Pallas kernels, shards(): pl.pallas_call(kernel, out_shape=(jax.ShapeDtypeStruct((PTS, NORB), f32),...  139 us

profile of v2, /device:TPU:1, one launch (start us, length us, event | category | flops | bytes accessed | tf_op | source)
XLA Modules:
  0.0 141.5 jit_solution(16363341875467440406)
XLA Ops:
  0.6 139.2 %rotate.1 = (f32[3072,128]{1,0:T(8,128)S(1)}, f32[24,128]{1,0:T(8,128)S(1)}, f32[3072,128]{1,0:T(8,128)S(1)}, f32[1,128]{1,0:T(1,128)S(1)}) custom-call(f32[3072,128]{1,0:T(8,128)} %psi.1, f32[2048,128]{1,0:T(8,128)} %rot.1, f32[1,128]{1,0:T(1,128)} %bitcast.7, f32[24,128]{1,0:T(8,128)} %bitcast.6), custom_call_target="tpu_custom_call" | custom-call | tf_op jit(solution)/shard_map/rotate/pallas_call | solution.py:294
  139.8 1.7 %put.1 = (f32[3072,128]{1,0:T(8,128)}, f32[3072]{0:T(1024)}, f32[3072,128]{1,0:T(8,128)}, f32[128]{0:T(128)}) custom-call(f32[3072,128]{1,0:T(8,128)S(1)} %get-tuple-element.8.refs_0_, f32[3072]{0:T(1024)S(1)} %bitcast.4, f32[3072,128]{1,0:T(8,128)S(1)} %get-tuple-element.10.refs_2_, f32[128]{0:T(128)S(1)} %bitcast.5), custom_call_target="tpu_custom_call" | custom-call | tf_op jit(solution)/shard_map/put/pallas_call | solution.py:279

commit v3 on v2

v3 whole, which is shorter than its diff:
```python
import functools

import jax
import jax.numpy as jnp
from jax import lax
from jax.experimental import pallas as pl
from jax.experimental.pallas import tpu as pltpu
from jax.sharding import PartitionSpec as P

M = 2048
PTS = 3072
NORB = 128
NLINE = 24
LINE = 128
NPTS = 49152
N = 12
HALF = N * LINE
AHEAD1 = 3
AHEAD2 = 4
LAG_1 = 2
HOP = 1
DONE_1 = LAG_1 + 3 * HOP
LAG_2 = 3
DONE_2 = 4
MESH = pl.DeviceIdType.MESH
HIGHEST = lax.Precision.HIGHEST


def line_2(k):
    return k + 16 - 12 * (k // 8)


def split(v):
    hi = v.astype(jnp.bfloat16)
    return hi, (v - hi.astype(jnp.float32)).astype(jnp.bfloat16)


def cbrt(d):
    safe = jnp.maximum(d, 1e-37)
    y = jnp.exp(jnp.log(safe) * (1.0 / 3.0))
    y = y - (y - safe / (y * y)) * (1.0 / 3.0)
    return jnp.where(d < 1e-37, 0.0, y)


def kernel(psi, rot, occ_hbm, vloc_hbm, rotated, dens, hpsi, band,
           occ, vloc, a1, a2, rotv, rb1, rb2, b1hi, b1lo, b2hi, b2lo, q, into_r, into_l, p2, rs2, halo, dpart, dx, bpart, bx,
           in_sem, a1_recv, a1_send, a2_recv, a2_send, r1_send, r1_recv, s1_send, s1_recv, r2_send, r2_recv, s2_sem,
           r_recv, r_send, l_recv, l_send, rs_recv, rs_send, h_recv, h_send, d_send, d_recv, b_send, b_recv):
    dom = lax.axis_index("dom")
    orb = lax.axis_index("orb")
    y, zh, c = dom // 4, (dom // 2) % 2, dom % 2
    z, x = orb // 4, orb % 4
    at_right, at_left = (dom, ((z + 1) % 4) * 4 + x), (dom, ((z + 3) % 4) * 4 + x)
    at_prev, at_next = ((dom + 15) % 16, orb), ((dom + 1) % 16, orb)
    at_twin = (dom + 1 - 2 * c, orb)
    e = y * 2 + c

    def at_yc(f):
        return ((f // 2) * 4 + zh * 2 + f % 2, orb)

    x_peers = [(dom, z * 4 + (x + j) % 4) for j in (1, 2, 3)]
    z_peers = [(dom, ((z + j) % 4) * 4 + x) for j in (1, 2, 3)]
    orb_peers = [(dom, (orb + j) % 16) for j in range(1, 16)]
    dom_peers = [((dom + j) % 16, orb) for j in range(1, 16)]
    yc_peers = [at_yc((e + j) % 8) for j in range(1, 8)]

    loads = [pltpu.make_async_copy(src, dst, in_sem.at[n]) for n, (src, dst) in enumerate([
        (psi.at[pl.ds(0, HALF)], a1.at[x]),
        (psi.at[pl.ds(2048, 1024)], a2.at[z, pl.ds(0, 1024)]),
        (psi.at[pl.ds(HALF, 512)], a2.at[z, pl.ds(1024, 512)]),
        (rot, rotv), (occ_hbm, occ), (vloc_hbm, vloc)])]
    for load in loads:
        load.start()

    barrier = pltpu.get_barrier_semaphore()
    everyone = orb_peers + dom_peers
    for peer in everyone:
        pl.semaphore_signal(barrier, inc=1, device_id=peer, device_id_type=MESH)
    pl.semaphore_wait(barrier, len(everyone))
    for load in loads:
        load.wait()

    def remote(src, dst, send, recv, peer):
        return pltpu.make_async_remote_copy(
            src_ref=src, dst_ref=dst, send_sem=send, recv_sem=recv, device_id=peer, device_id_type=MESH)

    def at(n, size):
        return pl.ds(pl.multiple_of(n * size, size), size)

    def send_1(k):
        ref = a1.at[x, at(k, LINE)]
        for j in range(3):
            remote(ref, ref, a1_send.at[j], a1_recv.at[x, k], x_peers[j]).start()

    def block_2(b, k, way):
        ref = a2.at[b, at(k, LINE)]
        return remote(ref, ref, a2_send.at[way, b], a2_recv.at[b, k], at_left if way else at_right)

    def got_2(b, k):
        block_2(b, k, 0).wait_recv()

    def send_2(k):
        @pl.when(z < 3)
        def _():
            block_2(z, k, 0).start()

        @pl.when(z > 0)
        def _():
            block_2(z, k, 1).start()

    def rot_1(j):
        return remote(rotv.at[at(((z + j + 1) % 4) * 8 + e, 64)], rb1.at[e, 2 - j],
                      r1_send.at[j], r1_recv.at[2 - j], z_peers[j])

    def share_1(j):
        return remote(rb1.at[e], rb1.at[e], s1_send.at[j], s1_recv.at[e], yc_peers[j])

    def rot_2(j, n):
        return remote(rotv.at[at((2 * c + n) * 4 + (x + j + 1) % 4, 128)], rb2.at[c, 2 - j, n],
                      r2_send.at[j, n], r2_recv.at[2 - j, n], x_peers[j])

    share_2 = remote(rb2.at[c], rb2.at[c], s2_sem.at[0], s2_sem.at[1], at_twin)

    send_2(0)
    for j in range(3):
        rot_1(j).start()
    for j in range(3):
        for n in range(2):
            rot_2(j, n).start()
    for k in range(1, AHEAD2):
        send_2(k)
    for k in range(AHEAD1):
        send_1(k)

    def onward(t, k, way):
        rows = at(k, LINE)
        if way == 0:
            return remote(q.at[t, rows], into_r.at[t, rows], r_send.at[t], r_recv.at[t, k], at_right)
        return remote(q.at[t, rows], into_l.at[t, rows], l_send.at[t], l_recv.at[t, k], at_left)

    def rs_2(j, k):
        rows = at(k, LINE)
        return remote(p2.at[(x + j + 1) % 4, rows], rs2.at[2 - j, rows], rs_send.at[j], rs_recv.at[2 - j, k], x_peers[j])

    def to_all(src, dst, send, recv, peers):
        for j, peer in enumerate(peers):
            remote(src, dst.at[14 - j], send, recv, peer).start()

    def from_all(dst, send, recv, peers):
        return remote(dst, dst, send, recv, peers[0])

    def plane_sums(p):
        to_all(dpart.at[pl.ds(p * 8, 8)], dx.at[p], d_send.at[p], d_recv.at[p], orb_peers)

    def product(a, hi_ref, lo_ref):
        hi, lo = split(a)
        total = jnp.dot(hi, lo_ref[...], preferred_element_type=jnp.float32)
        total += jnp.dot(lo, hi_ref[...], preferred_element_type=jnp.float32)
        return total + jnp.dot(hi, hi_ref[...], preferred_element_type=jnp.float32)

    def finish(r, line):
        rotated[at(line, LINE), :] = r
        d = lax.dot_general(jnp.broadcast_to(occ[...], (8, NORB)), r * r, (((1,), (1,)), ((), ())),
                            precision=HIGHEST, preferred_element_type=jnp.float32)
        dpart[pl.ds(line, 1), :] = d[0:1]

    def valid(k):
        return (k >= 0) & (k < N)

    def step(i, _):
        @pl.when(i + AHEAD2 < N)
        def _():
            send_2(i + AHEAD2)

        @pl.when(i + AHEAD1 < N)
        def _():
            send_1(i + AHEAD1)

        for hop in (1, 2):
            k = i - hop + 1

            @pl.when(valid(k) & (z >= hop))
            def _(hop=hop, k=k):
                got_2(z - hop, k)

                @pl.when(z < 3)
                def _():
                    block_2(z - hop, k, 0).start()

            @pl.when(valid(k) & (z <= 3 - hop))
            def _(hop=hop, k=k):
                got_2(z + hop, k)

                @pl.when(z > 0)
                def _():
                    block_2(z + hop, k, 1).start()

        @pl.when(i == 0)
        def _():
            for j in range(3):
                rot_1(j).wait_recv()
            for j in range(7):
                share_1(j).start()

        @pl.when(i == 1)
        def _():
            for j in range(3):
                for n in range(2):
                    rot_2(j, n).wait_recv()
            share_2.start()

        @pl.when(i == LAG_2)
        def _():
            share_2.wait_recv()
            for n in range(4):
                hi, lo = split(rotv[at(n * 4 + x, 128), :])
                b2hi[pl.ds(n * 128, 128), at(x, 128)] = hi
                b2lo[pl.ds(n * 128, 128), at(x, 128)] = lo
            for j in range(3):
                hi, lo = split(rb2[:, j].reshape(512, NORB))
                b2hi[:, at((x + j + 1) % 4, 128)] = hi
                b2lo[:, at((x + j + 1) % 4, 128)] = lo

        @pl.when(i == LAG_1)
        def _():
            for j in range(1, 8):
                f = (e + j) % 8
                remote(rb1.at[f], rb1.at[f], s1_send.at[0], s1_recv.at[f], at_twin).wait_recv()
            hi, lo = split(rotv[at(z, 512), :])
            b1hi[:, at(z, 128)] = hi
            b1lo[:, at(z, 128)] = lo
            for j in range(3):
                hi, lo = split(rb1[:, j].reshape(512, NORB))
                b1hi[:, at((z + j + 1) % 4, 128)] = hi
                b1lo[:, at((z + j + 1) % 4, 128)] = lo

        k1 = i - LAG_1

        @pl.when(valid(k1))
        def _():
            for j in range(1, 4):
                b = (x + j) % 4
                ref = a1.at[b, at(k1, LINE)]
                remote(ref, ref, a1_send.at[0], a1_recv.at[b, k1], at_right).wait_recv()
            rows = at(k1, LINE)
            total = product(jnp.concatenate([a1[b, rows, :] for b in range(4)], axis=1), b1hi, b1lo)
            for t in range(4):
                q[t, rows, :] = total[:, t * 128:(t + 1) * 128]

        k_r, k_l = k1 - z * HOP, k1 - (3 - z) * HOP
        for t in range(4):
            for way, k, first, mine, into in ((0, k_r, z > 0, t > z, into_r), (1, k_l, z < 3, t < z, into_l)):
                @pl.when(valid(k) & first & mine)
                def _(t=t, way=way, k=k, into=into):
                    onward(t, k, way).wait_recv()
                    rows = at(k, LINE)
                    q[t, rows, :] = q[t, rows, :] + into[t, rows, :]

        k2 = i - LAG_2

        @pl.when(valid(k2))
        def _():
            @pl.when(z == 3)
            def _():
                got_2(0, k2)

            @pl.when(z == 0)
            def _():
                got_2(3, k2)

            rows = at(k2, LINE)
            total = product(jnp.concatenate([a2[b, rows, :] for b in range(4)], axis=1), b2hi, b2lo)
            for t in range(4):
                p2[t, rows, :] = total[:, t * 128:(t + 1) * 128]

        for t in range(4):
            for way, k, mine in ((0, k_r, (t > z) & (z < 3)), (1, k_l, (t < z) & (z > 0))):
                @pl.when(valid(k) & mine)
                def _(t=t, way=way, k=k):
                    onward(t, k, way).start()

        f1, f2 = i - DONE_1, i - DONE_2

        @pl.when((f1 >= 1) & (f1 < 9))
        def _():
            ref = at(f1 - 1, LINE)
            remote(rotated.at[ref], halo.at[1, ref], h_send.at[0], h_recv.at[1], at_prev).start()

        @pl.when((f2 >= 1) & (f2 < 9))
        def _():
            remote(rotated.at[at(f2 - 1 + 16, LINE)], halo.at[0, at(f2 - 1, LINE)],
                   h_send.at[1], h_recv.at[0], at_next).start()

        @pl.when(f1 == 8)
        def _():
            plane_sums(0)

        @pl.when(f2 == 8)
        def _():
            plane_sums(2)

        @pl.when(valid(f2))
        def _():
            rows = at(f2, LINE)
            for j in range(3):
                rs_2(j, f2).wait_recv()
            finish((p2[x, rows, :] + rs2[0, rows, :]) + (rs2[1, rows, :] + rs2[2, rows, :]), line_2(f2))

        @pl.when(valid(f1))
        def _():
            rows = at(f1, LINE)

            @pl.when(z > 0)
            def _():
                onward(z, f1, 0).wait_recv()
                q[z, rows, :] = q[z, rows, :] + into_r[z, rows, :]

            @pl.when(z < 3)
            def _():
                onward(z, f1, 1).wait_recv()
                q[z, rows, :] = q[z, rows, :] + into_l[z, rows, :]

            finish(q[z, rows, :], f1)

        @pl.when(valid(k2))
        def _():
            for j in range(3):
                rs_2(j, k2).start()

        return 0

    lax.fori_loop(0, N + DONE_1, step, 0)

    half = pl.ds(0, HALF)
    for j in range(3):
        remote(a1.at[x], a1.at[x], a1_send.at[j], a1_recv.at[0, 0], x_peers[j]).wait_send()
    for b in range(4):
        for way, out, on in ((0, (z < 3) & (b <= z), (z < 3) & (b > z)), (1, (z > 0) & (b >= z), (z > 0) & (b < z))):
            @pl.when(out)
            def _(b=b, way=way):
                remote(a2.at[b], a2.at[b], a2_send.at[way, b], a2_recv.at[0, 0], at_right).wait_send()

            @pl.when(on)
            def _(b=b, way=way):
                sem = l_send if way else r_send
                remote(q.at[b], q.at[b], sem.at[b], r_recv.at[0, 0], at_right).wait_send()

    plane_sums(1)

    remote(halo.at[0], halo.at[0], h_send.at[0], h_recv.at[0], at_next).wait_recv()
    remote(halo.at[1], halo.at[1], h_send.at[0], h_recv.at[1], at_next).wait_recv()

    for p in range(3):
        for line in range(8):
            rows = pl.ds(line * LINE, LINE)
            here = pl.ds((p * 8 + line) * LINE, LINE)
            r = rotated[here, :]
            total = rotated[pl.ds(((p - 1) * 8 + line) * LINE, LINE), :] if p > 0 else halo[0, rows, :]
            total += rotated[pl.ds(((p + 1) * 8 + line) * LINE, LINE), :] if p < 2 else halo[1, rows, :]
            total += rotated[pl.ds((p * 8 + (line + 1) % 8) * LINE, LINE), :]
            total += rotated[pl.ds((p * 8 + (line + 7) % 8) * LINE, LINE), :]
            total += pltpu.roll(r, 1, 0) + pltpu.roll(r, LINE - 1, 0)
            hpsi[here, :] = 3.0 * r - 0.5 * total

    sums = []
    for p in range(3):
        from_all(dx.at[p], d_send.at[p], d_recv.at[p], orb_peers).wait_recv()
        total = dpart[p * 8:p * 8 + 8]
        for j in range(15):
            total += dx[p, j]
        sums.append(total)
    density = jnp.concatenate(sums, axis=0) * (1.0 / M)
    dens[...] = density
    pot = vloc[...] - (3.0 / jnp.pi) ** (1.0 / 3.0) * cbrt(density)
    turned = jnp.concatenate([pot, jnp.zeros((LINE - NLINE, LINE), jnp.float32)], axis=0).T

    acc = jnp.zeros((8, NORB), jnp.float32)
    for n in range(NLINE):
        rows = pl.ds(n * LINE, LINE)
        r = rotated[rows, :]
        h = hpsi[rows, :] + jnp.broadcast_to(turned[:, n:n + 1], (LINE, NORB)) * r
        hpsi[rows, :] = h
        acc += jnp.sum((r * h).reshape(LINE // 8, 8, NORB), axis=0)
    bpart[...] = acc
    for p in range(3):
        from_all(dx.at[p], d_send.at[p], d_recv.at[p], orb_peers).wait_send()
    to_all(bpart, bx, b_send.at[0], b_recv.at[0], dom_peers)
    shared = from_all(bx, b_send.at[0], b_recv.at[0], dom_peers)
    shared.wait_recv()
    total = acc
    for j in range(15):
        total += bx[j]
    band[...] = jnp.sum(total, axis=0, keepdims=True) * (1.0 / NPTS)
    shared.wait_send()

    for j in range(3):
        rot_1(j).wait_send()
        for n in range(2):
            rot_2(j, n).wait_send()
        remote(p2.at[0], p2.at[0], rs_send.at[j], rs_recv.at[0, 0], x_peers[j]).wait_send()
    for j in range(7):
        share_1(j).wait_send()
    share_2.wait_send()
    for side in range(2):
        remote(halo.at[0], halo.at[0], h_send.at[side], h_recv.at[0], at_next).wait_send()


def put_kernel(*refs):
    count = len(refs) // 2
    sem = refs[-1]
    copies = [pltpu.make_async_copy(refs[n], refs[count + n], sem.at[n]) for n in range(count)]
    for copy in copies:
        copy.start()
    for copy in copies:
        copy.wait()


def put(*arrays):
    hbm = pl.BlockSpec(memory_space=pl.ANY)
    return pl.pallas_call(
        put_kernel,
        out_shape=tuple(jax.ShapeDtypeStruct(a.shape, a.dtype) for a in arrays),
        in_specs=[hbm] * len(arrays),
        out_specs=(hbm,) * len(arrays),
        scratch_shapes=[pltpu.SemaphoreType.DMA((len(arrays),))],
        compiler_params=pltpu.CompilerParams(vmem_limit_bytes=16 * 1024 * 1024),
        name="put",
    )(*arrays)


def shards(psi, rot, occ, v_loc):
    f32 = jnp.float32
    vmem, hbm = pl.BlockSpec(memory_space=pltpu.VMEM), pl.BlockSpec(memory_space=pltpu.HBM)
    dma = pltpu.SemaphoreType.DMA
    rotated, density, hpsi, band = pl.pallas_call(
        kernel,
        out_shape=(
            jax.ShapeDtypeStruct((PTS, NORB), f32),
            jax.ShapeDtypeStruct((NLINE, LINE), f32),
            jax.ShapeDtypeStruct((PTS, NORB), f32),
            jax.ShapeDtypeStruct((1, NORB), f32),
        ),
        in_specs=[hbm] * 4,
        out_specs=(vmem, vmem, vmem, vmem),
        scratch_shapes=[
            pltpu.VMEM((1, NORB), f32),
            pltpu.VMEM((NLINE, LINE), f32),
            pltpu.VMEM((4, HALF, NORB), f32),
            pltpu.VMEM((4, HALF, NORB), f32),
            pltpu.VMEM((M, NORB), f32),
            pltpu.VMEM((8, 3, 64, NORB), f32),
            pltpu.VMEM((2, 3, 2, 128, NORB), f32),
            pltpu.VMEM((512, 512), jnp.bfloat16),
            pltpu.VMEM((512, 512), jnp.bfloat16),
            pltpu.VMEM((512, 512), jnp.bfloat16),
            pltpu.VMEM((512, 512), jnp.bfloat16),
            pltpu.VMEM((4, HALF, NORB), f32),
            pltpu.VMEM((4, HALF, NORB), f32),
            pltpu.VMEM((4, HALF, NORB), f32),
            pltpu.VMEM((4, HALF, NORB), f32),
            pltpu.VMEM((3, HALF, NORB), f32),
            pltpu.VMEM((2, 1024, NORB), f32),
            pltpu.VMEM((NLINE, LINE), f32),
            pltpu.VMEM((3, 15, 8, LINE), f32),
            pltpu.VMEM((8, NORB), f32),
            pltpu.VMEM((15, 8, NORB), f32),
            dma((6,)),
            dma((4, N)),
            dma((3,)),
            dma((4, N)),
            dma((2, 4)),
            dma((3,)),
            dma((3,)),
            dma((7,)),
            dma((8,)),
            dma((3, 2)),
            dma((3, 2)),
            dma((2,)),
            dma((4, N)),
            dma((4,)),
            dma((4, N)),
            dma((4,)),
            dma((3, N)),
            dma((3,)),
            dma((2,)),
            dma((2,)),
            dma((3,)),
            dma((3,)),
            dma((1,)),
            dma((1,)),
        ],
        compiler_params=pltpu.CompilerParams(
            collective_id=0, has_side_effects=True, vmem_limit_bytes=40 * 1024 * 1024),
        name="rotate",
    )(*[pltpu.with_memory_space_constraint(v, pltpu.HBM) for v in (
        psi, rot, occ.reshape(1, NORB), v_loc.reshape(NLINE, LINE))])
    return put(rotated, density.reshape(PTS), hpsi, band.reshape(NORB))


def solution(mesh):
    placed = (P("dom", "orb"), P(None, "orb"), P("orb"), P("dom"))
    return jax.shard_map(
        shards,
        mesh=mesh,
        in_specs=placed,
        out_specs=(P("dom", "orb"), P("dom"), P("dom", "orb"), P("orb")),
        check_vma=False,
    )
```

time: 142 us -> 135 us (0.951)
  Pallas kernels: 141 us -> 134 us
    pallas_call x1, Pallas kernels: 139 us -> 133 us  [shards(): pl.pallas_call(kernel, out_shape=(jax.ShapeDtypeStruct((PTS, NORB), f32),...]
where the time goes in v3:
time: 135 us
  Pallas kernels  134 us (99%)
    pallas_call x1, Pallas kernels, shards(): pl.pallas_call(kernel, out_shape=(jax.ShapeDtypeStruct((PTS, NORB), f32),...  133 us

profile of v3, /device:TPU:1, one launch (start us, length us, event | category | flops | bytes accessed | tf_op | source)
XLA Modules:
  0.0 134.9 jit_solution(9030751662874813862)
XLA Ops:
  0.6 132.6 %rotate.1 = (f32[3072,128]{1,0:T(8,128)S(1)}, f32[24,128]{1,0:T(8,128)S(1)}, f32[3072,128]{1,0:T(8,128)S(1)}, f32[1,128]{1,0:T(1,128)S(1)}) custom-call(f32[3072,128]{1,0:T(8,128)} %psi.1, f32[2048,128]{1,0:T(8,128)} %rot.1, f32[1,128]{1,0:T(1,128)} %bitcast.7, f32[24,128]{1,0:T(8,128)} %bitcast.6), custom_call_target="tpu_custom_call" | custom-call | tf_op jit(solution)/shard_map/rotate/pallas_call | solution.py:435
  133.2 1.7 %put.1 = (f32[3072,128]{1,0:T(8,128)}, f32[3072]{0:T(1024)}, f32[3072,128]{1,0:T(8,128)}, f32[128]{0:T(128)}) custom-call(f32[3072,128]{1,0:T(8,128)S(1)} %get-tuple-element.8.refs_0_, f32[3072]{0:T(1024)S(1)} %bitcast.4, f32[3072,128]{1,0:T(8,128)S(1)} %get-tuple-element.10.refs_2_, f32[128]{0:T(128)S(1)} %bitcast.5), custom_call_target="tpu_custom_call" | custom-call | tf_op jit(solution)/shard_map/put/pallas_call | solution.py:420

commit v4 on v3

--- a/solution.py
+++ b/solution.py
@@ -1,5 +1,3 @@
-import functools
-
 import jax
 import jax.numpy as jnp
 from jax import lax
@@ -22,6 +20,9 @@
 DONE_1 = LAG_1 + 3 * HOP
 LAG_2 = 3
 DONE_2 = 4
+LATE_1 = 4
+LATE_2 = 5
+
 MESH = pl.DeviceIdType.MESH
 HIGHEST = lax.Precision.HIGHEST
 
@@ -281,14 +282,16 @@
 
         f1, f2 = i - DONE_1, i - DONE_2
 
-        @pl.when((f1 >= 1) & (f1 < 9))
-        def _():
-            ref = at(f1 - 1, LINE)
+        g1, g2 = f1 - LATE_1, f2 - LATE_2
+
+        @pl.when((g1 >= 0) & (g1 < 8))
+        def _():
+            ref = at(g1, LINE)
             remote(rotated.at[ref], halo.at[1, ref], h_send.at[0], h_recv.at[1], at_prev).start()
 
-        @pl.when((f2 >= 1) & (f2 < 9))
-        def _():
-            remote(rotated.at[at(f2 - 1 + 16, LINE)], halo.at[0, at(f2 - 1, LINE)],
+        @pl.when((g2 >= 0) & (g2 < 8))
+        def _():
+            remote(rotated.at[at(g2 + 16, LINE)], halo.at[0, at(g2, LINE)],
                    h_send.at[1], h_recv.at[0], at_next).start()
 
         @pl.when(f1 == 8)
@@ -329,7 +332,7 @@
 
         return 0
 
-    lax.fori_loop(0, N + DONE_1, step, 0)
+    lax.fori_loop(0, max(N + DONE_1, 8 + DONE_1 + LATE_1, 8 + DONE_2 + LATE_2), step, 0)
 
     half = pl.ds(0, HALF)
     for j in range(3):
@@ -362,25 +365,23 @@
             total += pltpu.roll(r, 1, 0) + pltpu.roll(r, LINE - 1, 0)
             hpsi[here, :] = 3.0 * r - 0.5 * total
 
-    sums = []
-    for p in range(3):
+    acc = jnp.zeros((8, NORB), jnp.float32)
+    for p in (0, 2, 1):
         from_all(dx.at[p], d_send.at[p], d_recv.at[p], orb_peers).wait_recv()
-        total = dpart[p * 8:p * 8 + 8]
+        eight = pl.ds(p * 8, 8)
+        density = dpart[eight, :]
         for j in range(15):
-            total += dx[p, j]
-        sums.append(total)
-    density = jnp.concatenate(sums, axis=0) * (1.0 / M)
-    dens[...] = density
-    pot = vloc[...] - (3.0 / jnp.pi) ** (1.0 / 3.0) * cbrt(density)
-    turned = jnp.concatenate([pot, jnp.zeros((LINE - NLINE, LINE), jnp.float32)], axis=0).T
-
-    acc = jnp.zeros((8, NORB), jnp.float32)
-    for n in range(NLINE):
-        rows = pl.ds(n * LINE, LINE)
-        r = rotated[rows, :]
-        h = hpsi[rows, :] + jnp.broadcast_to(turned[:, n:n + 1], (LINE, NORB)) * r
-        hpsi[rows, :] = h
-        acc += jnp.sum((r * h).reshape(LINE // 8, 8, NORB), axis=0)
+            density += dx[p, j]
+        density = density * (1.0 / M)
+        dens[eight, :] = density
+        pot = vloc[eight, :] - (3.0 / jnp.pi) ** (1.0 / 3.0) * cbrt(density)
+        turned = jnp.concatenate([pot, jnp.zeros((LINE - 8, LINE), jnp.float32)], axis=0).T
+        for n in range(8):
+            rows = pl.ds((p * 8 + n) * LINE, LINE)
+            r = rotated[rows, :]
+            h = hpsi[rows, :] + jnp.broadcast_to(turned[:, n:n + 1], (LINE, NORB)) * r
+            hpsi[rows, :] = h
+            acc += jnp.sum((r * h).reshape(LINE // 8, 8, NORB), axis=0)
     bpart[...] = acc
     for p in range(3):
         from_all(dx.at[p], d_send.at[p], d_recv.at[p], orb_peers).wait_send()

time: 135 us -> 132 us (0.978)
  Pallas kernels: 134 us -> 131 us
    pallas_call x1, Pallas kernels: 133 us -> 130 us  [shards(): pl.pallas_call(kernel, out_shape=(jax.ShapeDtypeStruct((PTS, NORB), f32),...]
where the time goes in v4:
time: 132 us
  Pallas kernels  131 us (99%)
    pallas_call x1, Pallas kernels, shards(): pl.pallas_call(kernel, out_shape=(jax.ShapeDtypeStruct((PTS, NORB), f32),...  130 us

profile of v4, /device:TPU:1, one launch (start us, length us, event | category | flops | bytes accessed | tf_op | source)
XLA Modules:
  0.0 131.9 jit_solution(1740266059529415409)
XLA Ops:
  0.6 129.5 %rotate.1 = (f32[3072,128]{1,0:T(8,128)S(1)}, f32[24,128]{1,0:T(8,128)S(1)}, f32[3072,128]{1,0:T(8,128)S(1)}, f32[1,128]{1,0:T(1,128)S(1)}) custom-call(f32[3072,128]{1,0:T(8,128)} %psi.1, f32[2048,128]{1,0:T(8,128)} %rot.1, f32[1,128]{1,0:T(1,128)} %bitcast.7, f32[24,128]{1,0:T(8,128)} %bitcast.6), custom_call_target="tpu_custom_call" | custom-call | tf_op jit(solution)/shard_map/rotate/pallas_call | solution.py:436
  130.2 1.7 %put.1 = (f32[3072,128]{1,0:T(8,128)}, f32[3072]{0:T(1024)}, f32[3072,128]{1,0:T(8,128)}, f32[128]{0:T(128)}) custom-call(f32[3072,128]{1,0:T(8,128)S(1)} %get-tuple-element.8.refs_0_, f32[3072]{0:T(1024)S(1)} %bitcast.4, f32[3072,128]{1,0:T(8,128)S(1)} %get-tuple-element.10.refs_2_, f32[128]{0:T(128)S(1)} %bitcast.5), custom_call_target="tpu_custom_call" | custom-call | tf_op jit(solution)/shard_map/put/pallas_call | solution.py:421

commit v5 on v4

--- a/solution.py
+++ b/solution.py
@@ -6,6 +6,7 @@
 from jax.sharding import PartitionSpec as P
 
 M = 2048
+TINY = 1.1754944e-38
 PTS = 3072
 NORB = 128
 NLINE = 24
@@ -37,10 +38,10 @@
 
 
 def cbrt(d):
-    safe = jnp.maximum(d, 1e-37)
+    safe = jnp.maximum(d, TINY)
     y = jnp.exp(jnp.log(safe) * (1.0 / 3.0))
     y = y - (y - safe / (y * y)) * (1.0 / 3.0)
-    return jnp.where(d < 1e-37, 0.0, y)
+    return jnp.where(d < TINY, 0.0, y)
 
 
 def kernel(psi, rot, occ_hbm, vloc_hbm, rotated, dens, hpsi, band,
@@ -169,14 +170,6 @@
         return (k >= 0) & (k < N)
 
     def step(i, _):
-        @pl.when(i + AHEAD2 < N)
-        def _():
-            send_2(i + AHEAD2)
-
-        @pl.when(i + AHEAD1 < N)
-        def _():
-            send_1(i + AHEAD1)
-
         for hop in (1, 2):
             k = i - hop + 1
 
@@ -279,6 +272,14 @@
                 @pl.when(valid(k) & mine)
                 def _(t=t, way=way, k=k):
                     onward(t, k, way).start()
+
+        @pl.when(i + AHEAD2 < N)
+        def _():
+            send_2(i + AHEAD2)
+
+        @pl.when(i + AHEAD1 < N)
+        def _():
+            send_1(i + AHEAD1)
 
         f1, f2 = i - DONE_1, i - DONE_2
 

time: 132 us -> 132 us (level)
  no operation moved by 1% of the time
where the time goes in v5:
time: 132 us
  Pallas kernels  131 us (99%)
    pallas_call x1, Pallas kernels, shards(): pl.pallas_call(kernel, out_shape=(jax.ShapeDtypeStruct((PTS, NORB), f32),...  129 us

profile of v5, /device:TPU:1, one launch (start us, length us, event | category | flops | bytes accessed | tf_op | source)
XLA Modules:
  0.0 131.7 jit_solution(15762058543202701515)
XLA Ops:
  0.6 129.3 %rotate.1 = (f32[3072,128]{1,0:T(8,128)S(1)}, f32[24,128]{1,0:T(8,128)S(1)}, f32[3072,128]{1,0:T(8,128)S(1)}, f32[1,128]{1,0:T(1,128)S(1)}) custom-call(f32[3072,128]{1,0:T(8,128)} %psi.1, f32[2048,128]{1,0:T(8,128)} %rot.1, f32[1,128]{1,0:T(1,128)} %bitcast.7, f32[24,128]{1,0:T(8,128)} %bitcast.6), custom_call_target="tpu_custom_call" | custom-call | tf_op jit(solution)/shard_map/rotate/pallas_call | solution.py:437
  130.0 1.7 %put.1 = (f32[3072,128]{1,0:T(8,128)}, f32[3072]{0:T(1024)}, f32[3072,128]{1,0:T(8,128)}, f32[128]{0:T(128)}) custom-call(f32[3072,128]{1,0:T(8,128)S(1)} %get-tuple-element.8.refs_0_, f32[3072]{0:T(1024)S(1)} %bitcast.4, f32[3072,128]{1,0:T(8,128)S(1)} %get-tuple-element.10.refs_2_, f32[128]{0:T(128)S(1)} %bitcast.5), custom_call_target="tpu_custom_call" | custom-call | tf_op jit(solution)/shard_map/put/pallas_call | solution.py:422

commit v6 on v5

--- a/solution.py
+++ b/solution.py
@@ -15,7 +15,7 @@
 N = 12
 HALF = N * LINE
 AHEAD1 = 3
-AHEAD2 = 4
+AHEAD2 = 5
 LAG_1 = 2
 HOP = 1
 DONE_1 = LAG_1 + 3 * HOP

time: 132 us -> 132 us (level)
  no operation moved by 1% of the time
where the time goes in v6:
time: 132 us
  Pallas kernels  131 us (99%)
    pallas_call x1, Pallas kernels, shards(): pl.pallas_call(kernel, out_shape=(jax.ShapeDtypeStruct((PTS, NORB), f32),...  130 us

profile of v6, /device:TPU:1, one launch (start us, length us, event | category | flops | bytes accessed | tf_op | source)
XLA Modules:
  0.0 131.8 jit_solution(7907515300631775907)
XLA Ops:
  0.6 129.5 %rotate.1 = (f32[3072,128]{1,0:T(8,128)S(1)}, f32[24,128]{1,0:T(8,128)S(1)}, f32[3072,128]{1,0:T(8,128)S(1)}, f32[1,128]{1,0:T(1,128)S(1)}) custom-call(f32[3072,128]{1,0:T(8,128)} %psi.1, f32[2048,128]{1,0:T(8,128)} %rot.1, f32[1,128]{1,0:T(1,128)} %bitcast.7, f32[24,128]{1,0:T(8,128)} %bitcast.6), custom_call_target="tpu_custom_call" | custom-call | tf_op jit(solution)/shard_map/rotate/pallas_call | solution.py:437
  130.1 1.7 %put.1 = (f32[3072,128]{1,0:T(8,128)}, f32[3072]{0:T(1024)}, f32[3072,128]{1,0:T(8,128)}, f32[128]{0:T(128)}) custom-call(f32[3072,128]{1,0:T(8,128)S(1)} %get-tuple-element.8.refs_0_, f32[3072]{0:T(1024)S(1)} %bitcast.4, f32[3072,128]{1,0:T(8,128)S(1)} %get-tuple-element.10.refs_2_, f32[128]{0:T(128)S(1)} %bitcast.5), custom_call_target="tpu_custom_call" | custom-call | tf_op jit(solution)/shard_map/put/pallas_call | solution.py:422
